TPU v7x, 512 devices: a whole 4x8x8 slice. The times are simulated.
512 devices in a mesh: pair: 16 (over z, core), virt: 32 (over x, y).
Axes of the slice: x: 4, y: 8, z: 8, core: 2. Of those that a mesh axis runs over, the one named last changes fastest.
Arguments:
- amplitudes: bfloat16 [1024, 512, 512], P('pair', 'virt')
- integrals: bfloat16 [8, 512, 512, 512], P(None, 'pair', 'virt')
- pair_occ: int32 [1024, 2], P('virt'), may hold values from 0 to 119, as said below
- occ_irrep: int32 [120], replicated, may hold values from 0 to 7, as said below
- virt_irrep: int32 [512], replicated, may hold values from 0 to 7, as said below
- occ_energy: float32 [120], replicated, may hold values from -3 to -0.5
- virt_energy: float32 [512], replicated, may hold values from 0.3 to 4
Outputs:
- update: float32 [1024, 8, 512], P('virt', None, 'pair')
Inputs may be any that keep to these rules, and one draw needn't show every extreme that they name: `pair_occ`: each row holds i < j, and rows are distinct. `occ_irrep`: labels of the D2h irreps; every label occurs. `virt_irrep`: labels of the D2h irreps; every label occurs.
All inputs are finite; a program needn't handle non-finite values.
Results may differ from a plain program's by a relative error of at most 0.0003.
Values may be sent and summed in bfloat16 or wider, within the bound.
A program may use at most 128 MiB of HBM per device.

v0:
```python
import jax
import jax.numpy as jnp
from jax import lax
from jax.sharding import PartitionSpec as P


def table_lookup(indices, table, zero_value):
    orbital = jnp.arange(table.shape[0], dtype=jnp.int32)
    hits = indices[:, None] == orbital[None, :]
    return jnp.sum(jnp.where(hits, table[None, :], zero_value), axis=1)


def local(amplitudes, integrals, pair_occ, occ_irrep, virt_irrep, occ_energy, virt_energy):
    window_size, local_width, local_depth, full_width = integrals.shape
    integral_matrix = integrals.reshape(window_size * local_width, local_depth * full_width)
    owned_rows = pair_occ.shape[0]
    block_rows = lax.all_gather(amplitudes, "pair", axis=0, tiled=True)
    flattened = block_rows.reshape(block_rows.shape[0], local_depth * full_width)
    partial_value = lax.dot_general(
        flattened, integral_matrix, (((1,), (1,)), ((), ())), preferred_element_type=jnp.float32
    )
    summed = lax.psum(partial_value, "virt")
    ladder = lax.dynamic_slice_in_dim(summed, lax.axis_index("virt") * owned_rows, owned_rows, 0)
    ladder = ladder.reshape(owned_rows, window_size, local_width)
    b_offset = lax.axis_index("pair") * local_width
    local_sym = lax.dynamic_slice_in_dim(virt_irrep, b_offset, local_width, 0)
    local_energy = lax.dynamic_slice_in_dim(virt_energy, b_offset, local_width, 0)
    first_occ = pair_occ[:, 0]
    second_occ = pair_occ[:, 1]
    pair_sym = jnp.bitwise_xor(
        table_lookup(first_occ, occ_irrep, 0), table_lookup(second_occ, occ_irrep, 0)
    )
    pair_energy = table_lookup(first_occ, occ_energy, 0.0) + table_lookup(
        second_occ, occ_energy, 0.0
    )
    window_sym = virt_irrep[:window_size]
    total_sym = jnp.bitwise_xor(
        pair_sym[:, None, None],
        jnp.bitwise_xor(window_sym[None, :, None], local_sym[None, None, :]),
    )
    allowed = total_sym == 0
    denom = (
        pair_energy[:, None, None]
        - virt_energy[:window_size][None, :, None]
        - local_energy[None, None, :]
    )
    return jnp.where(allowed, ladder / denom, jnp.zeros_like(ladder))


def solution(mesh):
    return jax.shard_map(
        local,
        mesh=mesh,
        in_specs=(
            P("pair", "virt", None),
            P(None, "pair", "virt", None),
            P("virt", None),
            P(),
            P(),
            P(),
            P(),
        ),
        out_specs=P("virt", None, "pair"),
        check_vma=False,
    )
```

profile of v0, /device:TPU:64, one launch (start us, length us, event | category | flops | bytes accessed | tf_op | source)
XLA Modules:
  0.0 301.6 jit_solution(1929621240613633479)
XLA Ops:
  6.5 0.0 all-gather.2.cloned.1.call-start
  6.5 0.7 all-gather.2.cloned.1.call-update
  7.3 0.0 all-reduce.2.cloned.1.call-start
  7.3 8.4 %copy.9 = bf16[32,8,16,512]{3,1,2,0:T(8,128)(2,1)} copy(bf16[32,8,16,512]{3,2,1,0:T(8,128)(2,1)} %bitcast.13) | data formatting | bytes 8388608
  15.7 94.0 %all-gather.2.cloned.1.call-done = bf16[1024,16,512]{2,1,0:T(8,128)(2,1)} async-done(((bf16[64,16,512]{2,1,0:T(8,128)(2,1)}), bf16[1024,16,512]{2,1,0:T(8,128)(2,1)}) %all-gather.2.cloned.1.call-update) | async-done | bytes 16777232 | tf_op jit(solution)/shard_map/all_gather | solution.py:17
  109.7 0.0 copy-start
  109.7 16.0 %copy.8 = bf16[128,8,16,512]{3,1,2,0:T(8,128)(2,1)S(1)} copy(bf16[128,8,16,512]{3,2,1,0:T(8,128)(2,1)} %bitcast.11) | data formatting | bytes 33554432
  125.7 0.0 copy-start.4
  125.7 0.0 copy-start.5
  125.7 0.0 copy-start.1
  125.8 0.0 copy-start.2
  125.8 0.0 copy-start.3
  125.8 0.0 slice-start.1
  125.8 0.0 slice-start
  125.8 0.0 copy-done
  125.8 5.5 %fusion = f32[1024,256]{1,0:T(8,128)} fusion(bf16[1024,8192]{1,0:T(8,128)(2,1)S(1)} %bitcast.12, bf16[256,8192]{1,0:T(8,128)(2,1)S(1)} %bitcast.14), kind=kOutput, calls=%fused_computation.13 | convolution fusion | flops 4294967296 | bytes 22020096 | tf_op jit(solution)/shard_map/dot_general | solution.py:19
  131.4 0.0 all-reduce.2.cloned.1.call-update
  131.4 0.0 copy-done.4
  131.4 0.1 dynamic_slice.11
  131.5 0.0 copy-done.5
  131.5 0.1 dynamic_slice.9
  131.5 0.0 copy-done.1
  131.6 0.0 copy-done.2
  131.6 0.2 select_reduce_fusion
  131.8 0.0 copy-done.3
  131.8 0.2 select_reduce_fusion.2
  132.0 0.0 slice-done.1
  132.0 0.1 broadcast_xor_fusion
  132.0 0.0 slice-done
  132.0 0.1 broadcast_subtract_fusion
  132.1 161.0 %all-reduce.2.cloned.1.call-done = f32[1024,256]{1,0:T(8,128)} async-done(((f32[1024,256]{1,0:T(8,128)}), f32[1024,256]{1,0:T(8,128)}) %all-reduce.2.cloned.1.call-update) | async-done | bytes 1048592 | tf_op jit(solution)/shard_map/psum | solution.py:22
  293.1 0.8 constant_dynamic-slice_fusion
  293.9 0.1 reshape.87
  294.0 0.8 divide_select_fusion
  (3 shorter events, 0.0 us)
Async XLA Ops:
  6.5 103.2 %all-gather.2.cloned.1.call-start = ((), (), s32[]{:S(2)}) async-start(), calls=%async_computation | async-start | bytes 17825792 | tf_op jit(solution)/shard_map/all_gather | solution.py:17
  7.3 285.9 %all-reduce.2.cloned.1.call-start = ((), (), s32[]{:S(2)}) async-start(), calls=%async_computation.1 | async-start | bytes 2097152 | tf_op jit(solution)/shard_map/psum | solution.py:22
  109.7 16.1 %copy-start = (bf16[32,8,16,512]{3,1,2,0:T(8,128)(2,1)S(1)}, bf16[32,8,16,512]{3,1,2,0:T(8,128)(2,1)}, u32[]{:S(2)}) copy-start(bf16[32,8,16,512]{3,1,2,0:T(8,128)(2,1)} %copy.9) | copy-start | bytes 12582916
  125.7 5.7 %copy-start.4 = (f32[512]{0:T(512)S(1)}, f32[512]{0:T(512)}, u32[]{:S(2)}) copy-start(f32[512]{0:T(512)} %param.13) | copy-start | bytes 6148
  125.7 5.7 %copy-start.5 = (s32[512]{0:T(512)S(1)}, s32[512]{0:T(512)}, u32[]{:S(2)}) copy-start(s32[512]{0:T(512)} %param.11) | copy-start | bytes 6148
  125.7 5.8 %copy-start.1 = (s32[32,2]{0,1:T(2,128)S(1)}, s32[32,2]{0,1:T(2,128)}, u32[]{:S(2)}) copy-start(s32[32,2]{0,1:T(2,128)} %param.9) | copy-start | bytes 772
  125.8 5.8 %copy-start.2 = (f32[120]{0:T(128)S(1)}, f32[120]{0:T(128)}, u32[]{:S(2)}) copy-start(f32[120]{0:T(128)} %param.12) | copy-start | bytes 1444
  125.8 6.0 %copy-start.3 = (s32[120]{0:T(128)S(1)}, s32[120]{0:T(128)}, u32[]{:S(2)}) copy-start(s32[120]{0:T(128)} %param.10) | copy-start | bytes 1444
  125.8 6.2 %slice-start.1 = ((s32[512]{0:T(512)}), s32[8]{0:T(128)S(1)}, s32[]{:S(2)}) async-start(s32[512]{0:T(512)} %param.11), calls=%async_computation.3 | async-start | bytes 1024 | tf_op jit(solution)/shard_map/slice | solution.py:36
  125.8 6.2 %slice-start = ((f32[512]{0:T(512)}), f32[8]{0:T(128)S(1)}, s32[]{:S(2)}) async-start(f32[512]{0:T(512)} %param.13), calls=%async_computation.2 | async-start | bytes 1024 | tf_op jit(solution)/shard_map/slice | solution.py:44
Sparse Core Ops, SparseCore 0:
  9.4 100.2 all-gather.1
  131.5 161.6 all-reduce.1
where the time goes:
time: 302 us
  waiting for transfers between devices  256 us (85%)
  local copies, waits for them, and re-layouts  25.5 us (8%)
  between operations  13.5 us (4%)
  matrix products  5.53 us (2%)
    psum x1, waiting for transfers between devices, local(): summed = lax.psum(partial_value, 'virt')  161 us
    all_gather x1, waiting for transfers between devices, local(): block_rows = lax.all_gather(amplitudes, 'pair', axis=0, tiled=True)  94 us
    unnamed x14, local copies, waits for them, and re-layouts  24.5 us
  transfers between devices with their start and end apart: 2, of which 2 were waited for; matrix products, arithmetic and copies ran while one was open for 3% of the time, Pallas kernels for 0%

commit v1 on v0

--- a/solution.py
+++ b/solution.py
@@ -1,7 +1,21 @@
+import functools
 import jax
 import jax.numpy as jnp
 from jax import lax
 from jax.sharding import PartitionSpec as P
+
+
+def _try_all_shards(buf, chip_axis):
+    sheets = []
+    for _ in range(jax.lax.psum(1, axis_name=chip_axis)):
+        sheets.append(buf)
+    front = jnp.concatenate(
+        jax.lax.all_to_all(jnp.stack(sheets), axis_name=chip_axis, split_axis=0, concat_axis=0), 0
+    )
+    return front
+
+
+work_grid = functools.partial(_try_all_shards, chip_axis="pair")
 
 
 def table_lookup(indices, table, zero_value):
@@ -14,7 +28,7 @@
     window_size, local_width, local_depth, full_width = integrals.shape
     integral_matrix = integrals.reshape(window_size * local_width, local_depth * full_width)
     owned_rows = pair_occ.shape[0]
-    block_rows = lax.all_gather(amplitudes, "pair", axis=0, tiled=True)
+    block_rows = work_grid(amplitudes)
     flattened = block_rows.reshape(block_rows.shape[0], local_depth * full_width)
     partial_value = lax.dot_general(
         flattened, integral_matrix, (((1,), (1,)), ((), ())), preferred_element_type=jnp.float32

time: 302 us -> 578 us (1.91)
  waiting for transfers between devices: 256 us -> 515 us
  starting transfers between devices: 0.04 us -> 10 us
  local copies, waits for them, and re-layouts: 25.5 us -> 32.4 us
    all_to_all x0 -> x1, waiting for transfers between devices: none -> 354 us  [_try_all_shards(): jax.lax.all_to_all(jnp.stack(sheets), axis_name=chip_axis, split_axis=0,...]
    all_gather x1 -> x0, waiting for transfers between devices: 94 us -> none  [local(): block_rows = lax.all_gather(amplitudes, 'pair', axis=0, tiled=True)]
    all_to_all x0 -> x1, starting transfers between devices: none -> 9.98 us  [_try_all_shards(): jax.lax.all_to_all(jnp.stack(sheets), axis_name=chip_axis, split_axis=0,...]
    another operation x0 -> x1, local copies, waits for them, and re-layouts: none -> 6.84 us  [_try_all_shards(): jnp.stack(sheets)]
  transfers between devices with their start and end apart: 2 -> 2, of which waited for: 2 -> 2; matrix products, arithmetic and copies ran while one was open for 3% -> 2% of each run, Pallas kernels for 0% -> 0%
where the time goes in v1:
time: 578 us
  waiting for transfers between devices  515 us (89%)
  local copies, waits for them, and re-layouts  32.4 us (6%)
  between operations  13.5 us (2%)
  starting transfers between devices  10 us (2%)
    all_to_all x1, waiting for transfers between devices, _try_all_shards(): jax.lax.all_to_all(jnp.stack(sheets), axis_name=chip_axis, split_axis=0,...  354 us
    psum x1, waiting for transfers between devices, local(): summed = lax.psum(partial_value, 'virt')  161 us
    unnamed x14, local copies, waits for them, and re-layouts  24.6 us
  transfers between devices with their start and end apart: 2, of which 2 were waited for; matrix products, arithmetic and copies ran while one was open for 2% of the time, Pallas kernels for 0%

profile of v1, /device:TPU:64, one launch (start us, length us, event | category | flops | bytes accessed | tf_op | source)
XLA Modules:
  0.0 577.8 jit_solution(1644711326187701061)
XLA Ops:
  6.5 6.8 %stack.2 = bf16[16,64,16,512]{3,2,1,0:T(8,128)(2,1)} broadcast(bf16[64,16,512]{2,1,0:T(8,128)(2,1)} %param.7), dimensions={1,2,3} | broadcast | bytes 17825792 | tf_op jit(solution)/shard_map/stack | solution.py:13
  13.4 10.0 %all-to-all-start = ((bf16[16,64,16,512]{3,2,1,0:T(8,128)(2,1)}), bf16[16,64,16,512]{3,2,1,0:T(8,128)(2,1)}, u32[]{:S(2)}, u32[]{:S(2)}) async-start(bf16[16,64,16,512]{3,2,1,0:T(8,128)(2,1)} %stack.2), calls=%async_computation | async-start | bytes 33554432 | tf_op jit(solution)/shard_map/all_to_all | solution.py:13
  23.4 0.0 all-reduce.2.cloned.1.call-start
  23.4 8.5 %copy.9 = bf16[32,8,16,512]{3,1,2,0:T(8,128)(2,1)} copy(bf16[32,8,16,512]{3,2,1,0:T(8,128)(2,1)} %bitcast.13) | data formatting | bytes 8388608
  31.9 354.2 %all-to-all-done = bf16[16,64,16,512]{3,2,1,0:T(8,128)(2,1)} async-done(((bf16[16,64,16,512]{3,2,1,0:T(8,128)(2,1)}), bf16[16,64,16,512]{3,2,1,0:T(8,128)(2,1)}, u32[]{:S(2)}, u32[]{:S(2)}) %all-to-all-start) | async-done | bytes 16777248 | tf_op jit(solution)/shard_map/all_to_all | solution.py:13
  386.1 0.0 copy-start
  386.2 16.0 %copy.8 = bf16[128,8,16,512]{3,1,2,0:T(8,128)(2,1)S(1)} copy(bf16[128,8,16,512]{3,2,1,0:T(8,128)(2,1)} %bitcast.3) | data formatting | bytes 33554432
  402.2 0.0 copy-start.4
  402.2 0.0 copy-start.5
  402.2 0.0 copy-start.1
  402.2 0.0 copy-start.2
  402.2 0.0 copy-start.3
  402.2 0.0 slice-start.1
  402.2 0.0 slice-start
  402.2 0.0 copy-done
  402.2 5.5 fusion
  407.8 0.0 all-reduce.2.cloned.1.call-update
  407.8 0.0 copy-done.4
  407.8 0.1 dynamic_slice.11
  407.9 0.0 copy-done.5
  407.9 0.1 dynamic_slice.9
  408.0 0.0 copy-done.1
  408.0 0.0 copy-done.2
  408.0 0.2 select_reduce_fusion
  408.2 0.0 copy-done.3
  408.2 0.2 select_reduce_fusion.2
  408.4 0.0 slice-done.1
  408.4 0.1 broadcast_xor_fusion
  408.5 0.0 slice-done
  408.5 0.1 broadcast_subtract_fusion
  408.6 160.8 %all-reduce.2.cloned.1.call-done = f32[1024,256]{1,0:T(8,128)} async-done(((f32[1024,256]{1,0:T(8,128)}), f32[1024,256]{1,0:T(8,128)}) %all-reduce.2.cloned.1.call-update) | async-done | bytes 1048592 | tf_op jit(solution)/shard_map/psum | solution.py:36
  569.3 0.8 constant_dynamic-slice_fusion
  570.1 0.1 reshape.85
  570.2 0.8 divide_select_fusion
  (3 shorter events, 0.0 us)
Async XLA Ops:
  13.4 372.8 %all-to-all-start = ((bf16[16,64,16,512]{3,2,1,0:T(8,128)(2,1)}), bf16[16,64,16,512]{3,2,1,0:T(8,128)(2,1)}, u32[]{:S(2)}, u32[]{:S(2)}) async-start(bf16[16,64,16,512]{3,2,1,0:T(8,128)(2,1)} %stack.2), calls=%async_computation | async-start | bytes 33554432 | tf_op jit(solution)/shard_map/all_to_all | solution.py:13
  23.4 546.0 %all-reduce.2.cloned.1.call-start = ((), (), s32[]{:S(2)}) async-start(), calls=%async_computation.1 | async-start | bytes 2097152 | tf_op jit(solution)/shard_map/psum | solution.py:36
  386.1 16.1 %copy-start = (bf16[32,8,16,512]{3,1,2,0:T(8,128)(2,1)S(1)}, bf16[32,8,16,512]{3,1,2,0:T(8,128)(2,1)}, u32[]{:S(2)}) copy-start(bf16[32,8,16,512]{3,1,2,0:T(8,128)(2,1)} %copy.9) | copy-start | bytes 12582916
  402.2 5.7 copy-start.4
  402.2 5.7 copy-start.5
  402.2 5.8 %copy-start.1 = (s32[32,2]{0,1:T(2,128)S(1)}, s32[32,2]{0,1:T(2,128)}, u32[]{:S(2)}) copy-start(s32[32,2]{0,1:T(2,128)} %param.9) | copy-start | bytes 772
  402.2 5.8 %copy-start.2 = (f32[120]{0:T(128)S(1)}, f32[120]{0:T(128)}, u32[]{:S(2)}) copy-start(f32[120]{0:T(128)} %param.12) | copy-start | bytes 1444
  402.2 6.0 %copy-start.3 = (s32[120]{0:T(128)S(1)}, s32[120]{0:T(128)}, u32[]{:S(2)}) copy-start(s32[120]{0:T(128)} %param.10) | copy-start | bytes 1444
  402.2 6.2 %slice-start.1 = ((s32[512]{0:T(512)}), s32[8]{0:T(128)S(1)}, s32[]{:S(2)}) async-start(s32[512]{0:T(512)} %param.11), calls=%async_computation.3 | async-start | bytes 1024 | tf_op jit(solution)/shard_map/slice | solution.py:50
  402.2 6.3 %slice-start = ((f32[512]{0:T(512)}), f32[8]{0:T(128)S(1)}, s32[]{:S(2)}) async-start(f32[512]{0:T(512)} %param.13), calls=%async_computation.2 | async-start | bytes 1024 | tf_op jit(solution)/shard_map/slice | solution.py:58
Sparse Core Ops, SparseCore 0:
  407.9 161.3 all-reduce.1

commit v2 on v0

--- a/solution.py
+++ b/solution.py
@@ -19,7 +19,12 @@
     partial_value = lax.dot_general(
         flattened, integral_matrix, (((1,), (1,)), ((), ())), preferred_element_type=jnp.float32
     )
-    summed = lax.psum(partial_value, "virt")
+    dev_n = jax.lax.axis_size("virt")
+    summed = partial_value
+    for dd in [to_i for to_i in (1, 2, 4, 8, 16) if to_i < dev_n]:
+        summed = summed + jax.lax.ppermute(
+            summed, "virt", perm=tuple(((idx, idx ^ dd) for idx in range(dev_n)))
+        )
     ladder = lax.dynamic_slice_in_dim(summed, lax.axis_index("virt") * owned_rows, owned_rows, 0)
     ladder = ladder.reshape(owned_rows, window_size, local_width)
     b_offset = lax.axis_index("pair") * local_width

time: 302 us -> 325 us (1.076)
  the two profiles are of different devices: /device:TPU:64 before, /device:TPU:26 now
where the time goes in v2:
time: 325 us
  waiting for transfers between devices  264 us (81%)
  local copies, waits for them, and re-layouts  24.7 us (8%)
  starting transfers between devices  16 us (5%)
  between operations  13.6 us (4%)
  matrix products  4.53 us (1%)
    ppermute x5, waiting for transfers between devices, local(): jax.lax.ppermute(summed, 'virt', perm=tuple(((idx, idx ^ dd) for idx in r...  167 us
    all_gather x1, waiting for transfers between devices, local(): block_rows = lax.all_gather(amplitudes, 'pair', axis=0, tiled=True)  96.9 us
    unnamed x14, local copies, waits for them, and re-layouts  24.5 us
    ppermute x5, starting transfers between devices, local(): jax.lax.ppermute(summed, 'virt', perm=tuple(((idx, idx ^ dd) for idx in r...  16 us
  transfers between devices with their start and end apart: 6, of which 6 were waited for; matrix products, arithmetic and copies ran while one was open for 3% of the time, Pallas kernels for 0%

profile of v2, /device:TPU:26, one launch (start us, length us, event | category | flops | bytes accessed | tf_op | source)
XLA Modules:
  0.0 324.9 jit_solution(14396882831817059738)
XLA Ops:
  6.5 0.0 all-gather.2.cloned.1.call-start
  6.5 0.7 all-gather.2.cloned.1.call-update
  7.3 8.4 %copy.9 = bf16[32,8,16,512]{3,1,2,0:T(8,128)(2,1)} copy(bf16[32,8,16,512]{3,2,1,0:T(8,128)(2,1)} %bitcast.13) | data formatting | bytes 8388608
  15.7 96.9 %all-gather.2.cloned.1.call-done = bf16[1024,16,512]{2,1,0:T(8,128)(2,1)} async-done(((bf16[64,16,512]{2,1,0:T(8,128)(2,1)}), bf16[1024,16,512]{2,1,0:T(8,128)(2,1)}) %all-gather.2.cloned.1.call-update) | async-done | bytes 16777232 | tf_op jit(solution)/shard_map/all_gather | solution.py:17
  112.6 0.0 copy-start
  112.6 16.0 %copy.8 = bf16[128,8,16,512]{3,1,2,0:T(8,128)(2,1)S(1)} copy(bf16[128,8,16,512]{3,2,1,0:T(8,128)(2,1)} %bitcast.11) | data formatting | bytes 33554432
  128.6 0.0 copy-done
  128.6 0.0 copy-start.5
  128.7 0.0 copy-start.4
  128.7 0.0 copy-start.1
  128.7 0.0 copy-start.2
  128.7 0.0 copy-start.3
  128.7 0.0 slice-start.1
  128.7 0.0 slice-start
  128.7 4.5 %fusion = f32[1024,256]{1,0:T(8,128)S(1)} fusion(bf16[1024,8192]{1,0:T(8,128)(2,1)S(1)} %bitcast.12, bf16[256,8192]{1,0:T(8,128)(2,1)S(1)} %bitcast.14), kind=kOutput, calls=%fused_computation.13 | convolution fusion | flops 4294967296 | bytes 22020096 | tf_op jit(solution)/shard_map/dot_general | solution.py:19
  133.3 2.4 collective-permute-start
  135.7 24.8 %collective-permute-done = f32[1024,256]{1,0:T(8,128)S(1)} collective-permute-done((f32[1024,256]{1,0:T(8,128)S(1)}, f32[1024,256]{1,0:T(8,128)S(1)}, u32[]{:S(2)}, u32[]{:S(2)}) %collective-permute-start) | collective-permute-done | bytes 1048608 | tf_op jit(solution)/shard_map/ppermute | solution.py:25
  160.5 0.1 add.30
  160.6 2.4 collective-permute-start.1
  163.0 47.3 %collective-permute-done.1 = f32[1024,256]{1,0:T(8,128)S(1)} collective-permute-done((f32[1024,256]{1,0:T(8,128)S(1)}, f32[1024,256]{1,0:T(8,128)S(1)}, u32[]{:S(2)}, u32[]{:S(2)}) %collective-permute-start.1) | collective-permute-done | bytes 1048608 | tf_op jit(solution)/shard_map/ppermute | solution.py:25
  210.3 0.1 add.31
  210.4 4.7 %collective-permute-start.2 = (f32[1024,256]{1,0:T(8,128)S(1)}, f32[1024,256]{1,0:T(8,128)S(1)}, u32[]{:S(2)}, u32[]{:S(2)}) collective-permute-start(f32[1024,256]{1,0:T(8,128)S(1)} %add.31), channel_id=1, source_target_pairs={{0,4},{1,5},{2,6},{3,7},{4,0},{5,1},{6,2},{7,3},{8,12},{9,13},{10,... | collective-permute-start | bytes 3145736 | tf_op jit(solution)/shard_map/ppermute | solution.py:25
  215.1 47.2 %collective-permute-done.2 = f32[1024,256]{1,0:T(8,128)S(1)} collective-permute-done((f32[1024,256]{1,0:T(8,128)S(1)}, f32[1024,256]{1,0:T(8,128)S(1)}, u32[]{:S(2)}, u32[]{:S(2)}) %collective-permute-start.2) | collective-permute-done | bytes 1048608 | tf_op jit(solution)/shard_map/ppermute | solution.py:25
  262.4 0.1 add.32
  262.5 2.5 collective-permute-start.3
  265.0 24.5 %collective-permute-done.3 = f32[1024,256]{1,0:T(8,128)S(1)} collective-permute-done((f32[1024,256]{1,0:T(8,128)S(1)}, f32[1024,256]{1,0:T(8,128)S(1)}, u32[]{:S(2)}, u32[]{:S(2)}) %collective-permute-start.3) | collective-permute-done | bytes 1048608 | tf_op jit(solution)/shard_map/ppermute | solution.py:25
  289.4 0.1 add.33
  289.6 4.0 %collective-permute-start.4 = (f32[1024,256]{1,0:T(8,128)S(1)}, f32[1024,256]{1,0:T(8,128)S(1)}, u32[]{:S(2)}, u32[]{:S(2)}) collective-permute-start(f32[1024,256]{1,0:T(8,128)S(1)} %add.33), channel_id=1, source_target_pairs={{0,16},{1,17},{2,18},{3,19},{4,20},{5,21},{6,22},{7,23},{8,24},{9,... | collective-permute-start | bytes 3145736 | tf_op jit(solution)/shard_map/ppermute | solution.py:25
  293.6 0.0 copy-done.5
  293.6 0.1 dynamic_slice.9
  293.7 0.0 copy-done.4
  293.7 0.1 dynamic_slice.11
  293.7 0.0 copy-done.1
  293.7 0.0 copy-done.2
  293.8 0.2 select_reduce_fusion
  293.9 0.0 copy-done.3
  294.0 0.2 select_reduce_fusion.2
  294.1 0.0 slice-done.1
  294.2 0.1 broadcast_xor_fusion
  294.2 0.0 slice-done
  294.2 0.1 broadcast_subtract_fusion
  294.3 22.9 %collective-permute-done.4 = f32[1024,256]{1,0:T(8,128)S(1)} collective-permute-done((f32[1024,256]{1,0:T(8,128)S(1)}, f32[1024,256]{1,0:T(8,128)S(1)}, u32[]{:S(2)}, u32[]{:S(2)}) %collective-permute-start.4) | collective-permute-done | bytes 1048608 | tf_op jit(solution)/shard_map/ppermute | solution.py:25
  317.2 0.1 reshape.87
  317.3 0.8 divide_select_fusion
  (4 shorter events, 0.0 us)
Async XLA Ops:
  6.5 106.1 %all-gather.2.cloned.1.call-start = ((), (), s32[]{:S(2)}) async-start(), calls=%async_computation | async-start | bytes 17825792 | tf_op jit(solution)/shard_map/all_gather | solution.py:17
  112.6 16.0 %copy-start = (bf16[32,8,16,512]{3,1,2,0:T(8,128)(2,1)S(1)}, bf16[32,8,16,512]{3,1,2,0:T(8,128)(2,1)}, u32[]{:S(2)}) copy-start(bf16[32,8,16,512]{3,1,2,0:T(8,128)(2,1)} %copy.9) | copy-start | bytes 12582916
  128.6 164.9 %copy-start.5 = (s32[512]{0:T(512)S(1)}, s32[512]{0:T(512)}, u32[]{:S(2)}) copy-start(s32[512]{0:T(512)} %param.11) | copy-start | bytes 6148
  128.7 165.0 %copy-start.4 = (f32[512]{0:T(512)S(1)}, f32[512]{0:T(512)}, u32[]{:S(2)}) copy-start(f32[512]{0:T(512)} %param.13) | copy-start | bytes 6148
  128.7 165.1 %copy-start.1 = (s32[32,2]{0,1:T(2,128)S(1)}, s32[32,2]{0,1:T(2,128)}, u32[]{:S(2)}) copy-start(s32[32,2]{0,1:T(2,128)} %param.9) | copy-start | bytes 772
  128.7 165.1 %copy-start.2 = (f32[120]{0:T(128)S(1)}, f32[120]{0:T(128)}, u32[]{:S(2)}) copy-start(f32[120]{0:T(128)} %param.12) | copy-start | bytes 1444
  128.7 165.3 %copy-start.3 = (s32[120]{0:T(128)S(1)}, s32[120]{0:T(128)}, u32[]{:S(2)}) copy-start(s32[120]{0:T(128)} %param.10) | copy-start | bytes 1444
  128.7 165.4 %slice-start.1 = ((s32[512]{0:T(512)}), s32[8]{0:T(128)S(1)}, s32[]{:S(2)}) async-start(s32[512]{0:T(512)} %param.11), calls=%async_computation.2 | async-start | bytes 1024 | tf_op jit(solution)/shard_map/slice | solution.py:41
  128.7 165.5 %slice-start = ((f32[512]{0:T(512)}), f32[8]{0:T(128)S(1)}, s32[]{:S(2)}) async-start(f32[512]{0:T(512)} %param.13), calls=%async_computation.1 | async-start | bytes 1024 | tf_op jit(solution)/shard_map/slice | solution.py:49
  133.3 27.2 %collective-permute-start = (f32[1024,256]{1,0:T(8,128)S(1)}, f32[1024,256]{1,0:T(8,128)S(1)}, u32[]{:S(2)}, u32[]{:S(2)}) collective-permute-start(f32[1024,256]{1,0:T(8,128)S(1)} %fusion), channel_id=1, source_target_pairs={{0,1},{1,0},{2,3},{3,2},{4,5},{5,4},{6,7},{7,6},{8,9},{9,8},{10,11... | collective-permute-start | bytes 3145736 | tf_op jit(solution)/shard_map/ppermute | solution.py:25
  160.6 49.7 %collective-permute-start.1 = (f32[1024,256]{1,0:T(8,128)S(1)}, f32[1024,256]{1,0:T(8,128)S(1)}, u32[]{:S(2)}, u32[]{:S(2)}) collective-permute-start(f32[1024,256]{1,0:T(8,128)S(1)} %add.30), channel_id=1, source_target_pairs={{0,2},{1,3},{2,0},{3,1},{4,6},{5,7},{6,4},{7,5},{8,10},{9,11},{10,... | collective-permute-start | bytes 3145736 | tf_op jit(solution)/shard_map/ppermute | solution.py:25
  210.4 51.9 %collective-permute-start.2 = (f32[1024,256]{1,0:T(8,128)S(1)}, f32[1024,256]{1,0:T(8,128)S(1)}, u32[]{:S(2)}, u32[]{:S(2)}) collective-permute-start(f32[1024,256]{1,0:T(8,128)S(1)} %add.31), channel_id=1, source_target_pairs={{0,4},{1,5},{2,6},{3,7},{4,0},{5,1},{6,2},{7,3},{8,12},{9,13},{10,... | collective-permute-start | bytes 3145736 | tf_op jit(solution)/shard_map/ppermute | solution.py:25
  262.5 26.9 %collective-permute-start.3 = (f32[1024,256]{1,0:T(8,128)S(1)}, f32[1024,256]{1,0:T(8,128)S(1)}, u32[]{:S(2)}, u32[]{:S(2)}) collective-permute-start(f32[1024,256]{1,0:T(8,128)S(1)} %add.32), channel_id=1, source_target_pairs={{0,8},{1,9},{2,10},{3,11},{4,12},{5,13},{6,14},{7,15},{8,0},{9,1},... | collective-permute-start | bytes 3145736 | tf_op jit(solution)/shard_map/ppermute | solution.py:25
  289.6 27.6 %collective-permute-start.4 = (f32[1024,256]{1,0:T(8,128)S(1)}, f32[1024,256]{1,0:T(8,128)S(1)}, u32[]{:S(2)}, u32[]{:S(2)}) collective-permute-start(f32[1024,256]{1,0:T(8,128)S(1)} %add.33), channel_id=1, source_target_pairs={{0,16},{1,17},{2,18},{3,19},{4,20},{5,21},{6,22},{7,23},{8,24},{9,... | collective-permute-start | bytes 3145736 | tf_op jit(solution)/shard_map/ppermute | solution.py:25
Sparse Core Ops, SparseCore 0:
  9.4 103.1 all-gather.1
